TPU v7x, 32 devices: a whole 2x2x4 slice. The times are simulated.
32 devices in a mesh: clip: 2 (over x), tm: 4 (over z), chan: 4 (over y, core).
Axes of the slice: x: 2, y: 2, z: 4, core: 2. Of those that a mesh axis runs over, the one named last changes fastest.
Arguments:
- signal: bfloat16 [2, 4096, 256], P('clip', 'tm', 'chan'), may hold values from -6 to 6
- conv_first: bfloat16 [3, 256, 128], P(None, 'chan'), may hold values from -0.21875 to 0.21875
- conv_second: bfloat16 [128, 256], P(None, 'chan'), may hold values from -0.5 to 0.5
- conv_down: bfloat16 [16, 256, 512], P(None, 'chan'), may hold values from -0.09375 to 0.09375
- cotangent: bfloat16 [2, 512, 512], P('clip', 'tm'), may hold values from -6 to 6
Outputs:
- grad_signal: bfloat16 [2, 4096, 256], P('clip', 'tm', 'chan')
- grad_first: float32 [3, 256, 128], P(None, 'chan')
- grad_second: float32 [128, 256], P(None, 'chan')
- grad_down: float32 [16, 256, 512], P(None, 'chan')
All inputs are finite; a program needn't handle non-finite values.
Results may differ from a plain program's by a relative error of at most 0.018.
Values may be sent and summed in bfloat16 or wider, within the bound.
No kernel may reach another device: no remote copies, remote signals or barrier semaphores. Data moves between devices by JAX's collectives and lax.ppermute only.
A program may use at most 64 MiB of HBM per device.

v0:
```python
import jax
import jax.numpy as jnp
from jax import lax
from jax.sharding import PartitionSpec as P

KRES = 3
STRIDE = 8
RIM = 10


def shifted(block, axis, distance):
    devices = range(lax.axis_size(axis))
    route = [(i - distance, i) for i in devices if i - distance in devices]
    return lax.ppermute(block, axis, route)


def elu(value):
    return jnp.where(value > 0, value, jnp.exp(jnp.minimum(value, 0.0)) - 1.0)


def slope(value):
    return jnp.where(value > 0, 1.0, jnp.exp(jnp.minimum(value, 0.0)))


def contract_rows(left, right):
    return lax.dot_general(
        left, right, (((0,), (0,)), ((), ())), preferred_element_type=jnp.float32
    )


def contract_cols(left, right):
    return lax.dot_general(
        left, right, (((1,), (1,)), ((), ())), preferred_element_type=jnp.float32
    )


def causal_conv(values, weights, span):
    total = jnp.zeros((span, weights.shape[2]), jnp.float32)
    for k in range(KRES):
        total = total + jnp.dot(
            values[k : k + span], weights[k], preferred_element_type=jnp.float32
        )
    return total


def on_device(signal, conv_first, conv_second, conv_down, cotangent):
    frames = signal[0]
    length, local_ch = frames.shape
    span = length + RIM - KRES + 1
    borrowed = shifted(frames[length - RIM :], "tm", 1)
    padded = jnp.concatenate([borrowed, frames], axis=0)
    act = elu(padded.astype(jnp.float32)).astype(jnp.bfloat16)
    hidden = lax.psum(causal_conv(act, conv_first, span).astype(jnp.bfloat16), "chan").astype(
        jnp.float32
    )
    inner = elu(hidden).astype(jnp.bfloat16)
    resid = padded[KRES - 1 :].astype(jnp.float32) + jnp.dot(
        inner, conv_second, preferred_element_type=jnp.float32
    )
    feed = elu(resid).astype(jnp.bfloat16)
    blocks = feed.reshape(span // STRIDE, STRIDE * local_ch)
    wide = conv_down.reshape(2, STRIDE * local_ch, conv_down.shape[2])
    upstream = cotangent[0]
    count = upstream.shape[0]
    front = contract_cols(upstream, wide[0])
    back = contract_cols(upstream, wide[1])
    dblocks = jnp.pad(front, ((0, 1), (0, 0))) + jnp.pad(back, ((1, 0), (0, 0)))
    down_raw = jnp.stack(
        [contract_rows(blocks[:count], upstream), contract_rows(blocks[1:], upstream)]
    )
    down_raw = down_raw.reshape(conv_down.shape)
    dresid = dblocks.reshape(span, local_ch) * slope(resid)
    dres16 = dresid.astype(jnp.bfloat16)
    second_raw = contract_rows(inner, dres16)
    dinner = lax.psum(contract_cols(dres16, conv_second).astype(jnp.bfloat16), "chan").astype(
        jnp.float32
    )
    dhid = (dinner * slope(hidden)).astype(jnp.bfloat16)
    first_raw = jnp.stack([contract_rows(act[k : k + span], dhid) for k in range(KRES)])
    dact = jnp.zeros(padded.shape, jnp.float32)
    for k in range(KRES):
        dact = dact + jnp.pad(contract_cols(dhid, conv_first[k]), ((k, KRES - 1 - k), (0, 0)))
    dpadded = dact * slope(padded.astype(jnp.float32)) + jnp.pad(dresid, ((KRES - 1, 0), (0, 0)))
    returned = shifted(dpadded[:RIM], "tm", -1)
    grad_frames = dpadded[RIM:] + jnp.pad(returned, ((length - RIM, 0), (0, 0)))
    first_total, second_total, down_total = lax.psum(
        (first_raw, second_raw, down_raw), ("clip", "tm")
    )
    factor = 1.0 / jnp.sqrt(
        jnp.float32(lax.axis_size("clip") * lax.axis_size("tm") * (length // STRIDE))
    )
    return (
        grad_frames.astype(jnp.bfloat16)[None],
        first_total * factor,
        second_total * factor,
        down_total * factor,
    )


def solution(mesh):
    return jax.shard_map(
        on_device,
        mesh=mesh,
        in_specs=(
            P("clip", "tm", "chan"),
            P(None, "chan", None),
            P(None, "chan"),
            P(None, "chan", None),
            P("clip", "tm", None),
        ),
        out_specs=(
            P("clip", "tm", "chan"),
            P(None, "chan", None),
            P(None, "chan"),
            P(None, "chan", None),
        ),
        check_vma=False,
    )
```

profile of v0, /device:TPU:0, one launch (start us, length us, event | category | flops | bytes accessed | tf_op | source)
XLA Modules:
  0.0 208.7 jit_solution(13187131113075802272)
XLA Ops:
  7.2 0.9 slice_bitcast_fusion
  8.1 4.9 %collective-permute-start = (bf16[10,64]{0,1:T(8,128)(2,1)S(1)}, bf16[10,64]{0,1:T(8,128)(2,1)S(1)}, u32[]{:S(2)}, u32[]{:S(2)}) collective-permute-start(bf16[10,64]{0,1:T(8,128)(2,1)S(1)} %slice_bitcast_fusion), channel_id=1, source_target_pairs={{0,4},{4,8},{8,12},{1,5},{5,9},{9,13},{2,6},{6,10},{10,14},{3,7},{... | collective-permute-start | bytes 3848 | tf_op jit(solution)/shard_map/ppermute | solution.py:14
  13.0 1.3 fusion.56
  14.8 0.3 fusion.29
  15.2 0.5 convolution_add_fusion.1
  15.6 1.2 fusion
  17.6 32.4 %all-reduce.12.cloned.1.call-done = bf16[1032,128]{1,0:T(8,128)(2,1)} async-done(((bf16[1032,128]{1,0:T(8,128)(2,1)}), bf16[1032,128]{1,0:T(8,128)(2,1)}) %all-reduce.12.cloned.1.call-update) | async-done | bytes 264208 | tf_op jit(solution)/shard_map/psum | solution.py:53
  50.0 1.3 fusion.9
  52.2 1.0 convolution_convert_fusion
  53.3 0.3 convolution_bitcast_fusion
  53.6 0.3 convolution_bitcast_fusion.1
  54.0 1.5 pad_maximum_fusion
  55.4 30.2 %all-reduce.14.cloned.1.call-done = bf16[1032,128]{1,0:T(8,128)(2,1)} async-done(((bf16[1032,128]{1,0:T(8,128)(2,1)}), bf16[1032,128]{1,0:T(8,128)(2,1)}) %all-reduce.14.cloned.1.call-update) | async-done | bytes 264208 | tf_op jit(solution)/shard_map/psum | solution.py:75
  85.6 1.1 fusion.3
  87.4 0.7 pad_maximum_fusion.2
  88.4 39.2 %psum.38 = f32[128,64]{0,1:T(8,128)S(1)} all-reduce(f32[128,64]{0,1:T(8,128)S(1)} %fusion.31), channel_id=1, replica_groups=mesh['clip'=2,'tm'=4,'chan'=4] {'clip','tm'}, use_global_device_ids=true, to_apply=%region_3.4 | all-reduce | flops 8192 | bytes 65536 | tf_op jit(solution)/shard_map/psum | solution.py:86
  128.2 0.3 fusion.11
  128.6 1.3 collective-permute-start.1
  129.9 0.6 broadcast_multiply_fusion.2
  130.5 3.9 %collective-permute-done.1 = f32[10,64]{0,1:T(8,128)S(1)} collective-permute-done((f32[10,64]{0,1:T(8,128)S(1)}, f32[10,64]{0,1:T(8,128)S(1)}, u32[]{:S(2)}, u32[]{:S(2)}) %collective-permute-start.1) | collective-permute-done | bytes 2592 | tf_op jit(solution)/shard_map/ppermute | solution.py:14
  134.4 0.8 fusion.17
  135.2 62.3 %all-reduce.16.cloned.1.call-done = (f32[3,64,128]{2,1,0:T(8,128)}, f32[16,64,512]{2,1,0:T(8,128)}) async-done(((f32[3,64,128]{2,1,0:T(8,128)}, f32[16,64,512]{2,1,0:T(8,128)}), (f32[3,64,128]{2,1,0:T(8,128)}, f32[16,64,512]{2,1,0:T(8,128)})) %all-reduce.16.cloned.1.call-update) | async-done | bytes 2195472 | tf_op jit(solution)/shard_map/psum | solution.py:86
  197.5 1.5 broadcast_multiply_fusion.1
  199.0 3.2 %broadcast_multiply_fusion = f32[16,64,512]{2,1,0:T(8,128)} fusion(f32[16,64,512]{2,1,0:T(8,128)} %get-tuple-element.5), kind=kLoop, calls=%fused_computation.10 | loop fusion | flops 524288 | bytes 4194304 | tf_op jit(solution)/shard_map/mul | solution.py:96
  (36 shorter events, 3.8 us)
Async XLA Ops:
  7.2 7.2 %copy-start = (bf16[1,128,512]{2,1,0:T(8,128)(2,1)S(1)}, bf16[1,128,512]{2,1,0:T(8,128)(2,1)}, u32[]{:S(2)}) copy-start(bf16[1,128,512]{2,1,0:T(8,128)(2,1)} %param.9) | copy-start | bytes 393220
  7.2 7.5 %copy-start.1 = (bf16[1,1024,64]{1,2,0:T(8,128)(2,1)S(1)}, bf16[1,1024,64]{1,2,0:T(8,128)(2,1)}, u32[]{:S(2)}) copy-start(bf16[1,1024,64]{1,2,0:T(8,128)(2,1)} %param.5) | copy-start | bytes 393220
  7.2 7.6 %copy-start.3 = (bf16[3,64,128]{2,1,0:T(8,128)(2,1)S(1)}, bf16[3,64,128]{2,1,0:T(8,128)(2,1)}, u32[]{:S(2)}) copy-start(bf16[3,64,128]{2,1,0:T(8,128)(2,1)} %param.6) | copy-start | bytes 147460
  7.2 42.8 %all-reduce.12.cloned.1.call-start = ((), (), s32[]{:S(2)}) async-start(), calls=%async_computation | async-start | bytes 528384 | tf_op jit(solution)/shard_map/psum | solution.py:53
  8.1 6.5 %collective-permute-start = (bf16[10,64]{0,1:T(8,128)(2,1)S(1)}, bf16[10,64]{0,1:T(8,128)(2,1)S(1)}, u32[]{:S(2)}, u32[]{:S(2)}) collective-permute-start(bf16[10,64]{0,1:T(8,128)(2,1)S(1)} %slice_bitcast_fusion), channel_id=1, source_target_pairs={{0,4},{4,8},{8,12},{1,5},{5,9},{9,13},{2,6},{6,10},{10,14},{3,7},{... | collective-permute-start | bytes 3848 | tf_op jit(solution)/shard_map/ppermute | solution.py:14
  15.6 34.4 %copy-start.4 = (bf16[128,64]{0,1:T(8,128)(2,1)S(1)}, bf16[128,64]{0,1:T(8,128)(2,1)}, u32[]{:S(2)}) copy-start(bf16[128,64]{0,1:T(8,128)(2,1)} %param.7) | copy-start | bytes 49156
  16.8 68.8 %all-reduce.14.cloned.1.call-start = ((), (), s32[]{:S(2)}) async-start(), calls=%async_computation.1 | async-start | bytes 528384 | tf_op jit(solution)/shard_map/psum | solution.py:75
  53.3 144.2 %all-reduce.16.cloned.1.call-start = ((), (), s32[]{:S(2)}) async-start(), calls=%async_computation.2 | async-start | bytes 4390912 | tf_op jit(solution)/shard_map/psum | solution.py:86
  53.9 31.7 %copy-start.2 = (bf16[1032,128]{1,0:T(8,128)(2,1)S(1)}, bf16[1032,128]{1,0:T(8,128)(2,1)}, u32[]{:S(2)}) copy-start(bf16[1032,128]{1,0:T(8,128)(2,1)} %all-reduce.12.cloned.1.call-done) | copy-start | bytes 792580
  128.6 5.8 %collective-permute-start.1 = (f32[10,64]{0,1:T(8,128)S(1)}, f32[10,64]{0,1:T(8,128)S(1)}, u32[]{:S(2)}, u32[]{:S(2)}) collective-permute-start(f32[10,64]{0,1:T(8,128)S(1)} %slice.82), channel_id=1, source_target_pairs={{4,0},{8,4},{12,8},{5,1},{9,5},{13,9},{6,2},{10,6},{14,10},{7,3},{... | collective-permute-start | bytes 7688 | tf_op jit(solution)/shard_map/ppermute | solution.py:14
Sparse Core Ops, SparseCore 0:
  16.9 32.9 all-reduce.11
  53.4 32.2 all-reduce.13
  90.0 107.4 all-reduce.15
where the time goes:
time: 209 us
  waiting for transfers between devices  129 us (62%)
  blocking collectives  39.2 us (19%)
  between operations  13.9 us (7%)
  other arithmetic  9.89 us (5%)
  matrix products  7.15 us (3%)
  starting transfers between devices  6.33 us (3%)
  local copies, waits for them, and re-layouts  3.4 us (2%)
    psum x1, waiting for transfers between devices, on_device(): lax.psum((first_raw, second_raw, down_raw), ('clip', 'tm'))  62.3 us
    psum x1, blocking collectives, on_device(): lax.psum((first_raw, second_raw, down_raw), ('clip', 'tm'))  39.2 us
    psum x1, waiting for transfers between devices, on_device(): lax.psum(causal_conv(act, conv_first, span).astype(jnp.bfloat16), 'chan')  32.4 us
    psum x1, waiting for transfers between devices, on_device(): lax.psum(contract_cols(dres16, conv_second).astype(jnp.bfloat16), 'chan')  30.2 us
    ppermute x2, starting transfers between devices, shifted(): return lax.ppermute(block, axis, route)  6.21 us
  transfers between devices with their start and end apart: 5, of which 4 were waited for; matrix products, arithmetic and copies ran while one was open for 3% of the time, Pallas kernels for 0%

commit v1 on v0

--- a/solution.py
+++ b/solution.py
@@ -6,6 +6,12 @@
 KRES = 3
 STRIDE = 8
 RIM = 10
+
+
+def _lay_sheet(xin, chip_axis, device_axis):
+    for to_i in (chip_axis, device_axis):
+        xin = jax.lax.psum(xin, to_i)
+    return xin
 
 
 def shifted(block, axis, distance):
@@ -83,8 +89,8 @@
     dpadded = dact * slope(padded.astype(jnp.float32)) + jnp.pad(dresid, ((KRES - 1, 0), (0, 0)))
     returned = shifted(dpadded[:RIM], "tm", -1)
     grad_frames = dpadded[RIM:] + jnp.pad(returned, ((length - RIM, 0), (0, 0)))
-    first_total, second_total, down_total = lax.psum(
-        (first_raw, second_raw, down_raw), ("clip", "tm")
+    first_total, second_total, down_total = _lay_sheet(
+        (first_raw, second_raw, down_raw), "tm", "clip"
     )
     factor = 1.0 / jnp.sqrt(
         jnp.float32(lax.axis_size("clip") * lax.axis_size("tm") * (length // STRIDE))

time: 209 us -> 259 us (1.24)
  waiting for transfers between devices: 129 us -> 192 us
  blocking collectives: 39.2 us -> 26 us
    psum x1 -> x2, waiting for transfers between devices: 62.3 us -> 125 us  [_lay_sheet(): xin = jax.lax.psum(xin, to_i)]
    psum x1 -> x2, blocking collectives: 39.2 us -> 26 us  [_lay_sheet(): xin = jax.lax.psum(xin, to_i)]
  transfers between devices with their start and end apart: 5 -> 6, of which waited for: 4 -> 5; matrix products, arithmetic and copies ran while one was open for 3% -> 3% of each run, Pallas kernels for 0% -> 0%
where the time goes in v1:
time: 259 us
  waiting for transfers between devices  192 us (74%)
  blocking collectives  26 us (10%)
  between operations  14 us (5%)
  other arithmetic  9.89 us (4%)
  matrix products  7.14 us (3%)
  starting transfers between devices  6.37 us (2%)
  local copies, waits for them, and re-layouts  3.39 us (1%)
    psum x2, waiting for transfers between devices, _lay_sheet(): xin = jax.lax.psum(xin, to_i)  125 us
    psum x1, waiting for transfers between devices, on_device(): lax.psum(causal_conv(act, conv_first, span).astype(jnp.bfloat16), 'chan')  32.4 us
    psum x1, waiting for transfers between devices, on_device(): lax.psum(contract_cols(dres16, conv_second).astype(jnp.bfloat16), 'chan')  30.2 us
    psum x2, blocking collectives, _lay_sheet(): xin = jax.lax.psum(xin, to_i)  26 us
    ppermute x2, starting transfers between devices, shifted(): return lax.ppermute(block, axis, route)  6.21 us
  transfers between devices with their start and end apart: 6, of which 5 were waited for; matrix products, arithmetic and copies ran while one was open for 3% of the time, Pallas kernels for 0%

profile of v1, /device:TPU:0, one launch (start us, length us, event | category | flops | bytes accessed | tf_op | source)
XLA Modules:
  0.0 258.8 jit_solution(11523423065642519106)
XLA Ops:
  7.2 0.9 slice_bitcast_fusion
  8.1 4.9 %collective-permute-start = (bf16[10,64]{0,1:T(8,128)(2,1)S(1)}, bf16[10,64]{0,1:T(8,128)(2,1)S(1)}, u32[]{:S(2)}, u32[]{:S(2)}) collective-permute-start(bf16[10,64]{0,1:T(8,128)(2,1)S(1)} %slice_bitcast_fusion), channel_id=1, source_target_pairs={{0,4},{4,8},{8,12},{1,5},{5,9},{9,13},{2,6},{6,10},{10,14},{3,7},{... | collective-permute-start | bytes 3848 | tf_op jit(solution)/shard_map/ppermute | solution.py:20
  13.0 1.3 fusion.56
  14.8 0.3 fusion.29
  15.2 0.5 convolution_add_fusion.1
  15.6 1.2 fusion
  17.6 32.4 %all-reduce.14.cloned.1.call-done = bf16[1032,128]{1,0:T(8,128)(2,1)} async-done(((bf16[1032,128]{1,0:T(8,128)(2,1)}), bf16[1032,128]{1,0:T(8,128)(2,1)}) %all-reduce.14.cloned.1.call-update) | async-done | bytes 264208 | tf_op jit(solution)/shard_map/psum | solution.py:59
  50.0 1.3 fusion.9
  52.2 1.0 convolution_convert_fusion
  53.9 1.5 pad_maximum_fusion
  55.4 30.2 %all-reduce.16.cloned.1.call-done = bf16[1032,128]{1,0:T(8,128)(2,1)} async-done(((bf16[1032,128]{1,0:T(8,128)(2,1)}), bf16[1032,128]{1,0:T(8,128)(2,1)}) %all-reduce.16.cloned.1.call-update) | async-done | bytes 264208 | tf_op jit(solution)/shard_map/psum | solution.py:81
  85.6 1.1 fusion.3
  87.4 0.7 pad_maximum_fusion.2
  88.1 92.1 %all-reduce.18.cloned.1.call-done = (f32[3,64,128]{2,1,0:T(8,128)}, f32[16,64,512]{2,1,0:T(8,128)}) async-done(((f32[3,64,128]{2,1,0:T(8,128)}, f32[16,64,512]{2,1,0:T(8,128)}), (f32[3,64,128]{2,1,0:T(8,128)}, f32[16,64,512]{2,1,0:T(8,128)})) %all-reduce.18.cloned.1.call-update) | async-done | bytes 2195472 | tf_op jit(solution)/shard_map/psum | solution.py:13
  180.6 16.8 %psum.60 = f32[128,64]{0,1:T(8,128)S(1)} all-reduce(f32[128,64]{0,1:T(8,128)S(1)} %fusion.31), channel_id=1, replica_groups=mesh['clip'=2,'tm'=4,'chan'=4] {'tm'}, use_global_device_ids=true, to_apply=%region_4.5 | all-reduce | flops 8192 | bytes 65536 | tf_op jit(solution)/shard_map/psum | solution.py:13
  197.4 9.2 %psum.61 = f32[128,64]{0,1:T(8,128)S(1)} all-reduce(f32[128,64]{0,1:T(8,128)S(1)} %psum.60), channel_id=1, replica_groups=mesh['clip'=2,'tm'=4,'chan'=4] {'clip'}, use_global_device_ids=true, to_apply=%region_5.6 | all-reduce | flops 8192 | bytes 65536 | tf_op jit(solution)/shard_map/psum | solution.py:13
  207.3 0.3 fusion.11
  207.6 1.3 collective-permute-start.1
  208.9 0.6 broadcast_multiply_fusion.2
  209.5 3.9 %collective-permute-done.1 = f32[10,64]{0,1:T(8,128)S(1)} collective-permute-done((f32[10,64]{0,1:T(8,128)S(1)}, f32[10,64]{0,1:T(8,128)S(1)}, u32[]{:S(2)}, u32[]{:S(2)}) %collective-permute-start.1) | collective-permute-done | bytes 2592 | tf_op jit(solution)/shard_map/ppermute | solution.py:20
  213.4 0.8 fusion.17
  214.2 33.3 %all-reduce.20.cloned.1.call-done = (f32[3,64,128]{2,1,0:T(8,128)}, f32[16,64,512]{2,1,0:T(8,128)}) async-done(((f32[3,64,128]{2,1,0:T(8,128)}, f32[16,64,512]{2,1,0:T(8,128)}), (f32[3,64,128]{2,1,0:T(8,128)}, f32[16,64,512]{2,1,0:T(8,128)})) %all-reduce.20.cloned.1.call-update) | async-done | bytes 2195472 | tf_op jit(solution)/shard_map/psum | solution.py:13
  247.5 1.5 broadcast_multiply_fusion.1
  249.1 3.2 %broadcast_multiply_fusion = f32[16,64,512]{2,1,0:T(8,128)} fusion(f32[16,64,512]{2,1,0:T(8,128)} %get-tuple-element.7), kind=kLoop, calls=%fused_computation.10 | loop fusion | flops 524288 | bytes 4194304 | tf_op jit(solution)/shard_map/mul | solution.py:102
  (40 shorter events, 4.5 us)
Async XLA Ops:
  7.2 7.2 %copy-start = (bf16[1,128,512]{2,1,0:T(8,128)(2,1)S(1)}, bf16[1,128,512]{2,1,0:T(8,128)(2,1)}, u32[]{:S(2)}) copy-start(bf16[1,128,512]{2,1,0:T(8,128)(2,1)} %param.9) | copy-start | bytes 393220
  7.2 7.5 %copy-start.1 = (bf16[1,1024,64]{1,2,0:T(8,128)(2,1)S(1)}, bf16[1,1024,64]{1,2,0:T(8,128)(2,1)}, u32[]{:S(2)}) copy-start(bf16[1,1024,64]{1,2,0:T(8,128)(2,1)} %param.5) | copy-start | bytes 393220
  7.2 7.6 %copy-start.3 = (bf16[3,64,128]{2,1,0:T(8,128)(2,1)S(1)}, bf16[3,64,128]{2,1,0:T(8,128)(2,1)}, u32[]{:S(2)}) copy-start(bf16[3,64,128]{2,1,0:T(8,128)(2,1)} %param.6) | copy-start | bytes 147460
  7.2 42.8 %all-reduce.14.cloned.1.call-start = ((), (), s32[]{:S(2)}) async-start(), calls=%async_computation | async-start | bytes 528384 | tf_op jit(solution)/shard_map/psum | solution.py:59
  8.1 6.5 %collective-permute-start = (bf16[10,64]{0,1:T(8,128)(2,1)S(1)}, bf16[10,64]{0,1:T(8,128)(2,1)S(1)}, u32[]{:S(2)}, u32[]{:S(2)}) collective-permute-start(bf16[10,64]{0,1:T(8,128)(2,1)S(1)} %slice_bitcast_fusion), channel_id=1, source_target_pairs={{0,4},{4,8},{8,12},{1,5},{5,9},{9,13},{2,6},{6,10},{10,14},{3,7},{... | collective-permute-start | bytes 3848 | tf_op jit(solution)/shard_map/ppermute | solution.py:20
  15.6 34.4 %copy-start.4 = (bf16[128,64]{0,1:T(8,128)(2,1)S(1)}, bf16[128,64]{0,1:T(8,128)(2,1)}, u32[]{:S(2)}) copy-start(bf16[128,64]{0,1:T(8,128)(2,1)} %param.7) | copy-start | bytes 49156
  16.8 68.8 %all-reduce.16.cloned.1.call-start = ((), (), s32[]{:S(2)}) async-start(), calls=%async_computation.1 | async-start | bytes 528384 | tf_op jit(solution)/shard_map/psum | solution.py:81
  53.2 127.0 %all-reduce.18.cloned.1.call-start = ((), (), s32[]{:S(2)}) async-start(), calls=%async_computation.2 | async-start | bytes 4390912 | tf_op jit(solution)/shard_map/psum | solution.py:13
  53.9 31.7 %copy-start.2 = (bf16[1032,128]{1,0:T(8,128)(2,1)S(1)}, bf16[1032,128]{1,0:T(8,128)(2,1)}, u32[]{:S(2)}) copy-start(bf16[1032,128]{1,0:T(8,128)(2,1)} %all-reduce.14.cloned.1.call-done) | copy-start | bytes 792580
  88.1 159.4 %all-reduce.20.cloned.1.call-start = ((), (), s32[]{:S(2)}) async-start(), calls=%async_computation.3 | async-start | bytes 4390912 | tf_op jit(solution)/shard_map/psum | solution.py:13
  207.6 5.8 %collective-permute-start.1 = (f32[10,64]{0,1:T(8,128)S(1)}, f32[10,64]{0,1:T(8,128)S(1)}, u32[]{:S(2)}, u32[]{:S(2)}) collective-permute-start(f32[10,64]{0,1:T(8,128)S(1)} %slice.82), channel_id=1, source_target_pairs={{4,0},{8,4},{12,8},{5,1},{9,5},{13,9},{6,2},{10,6},{14,10},{7,3},{... | collective-permute-start | bytes 7688 | tf_op jit(solution)/shard_map/ppermute | solution.py:20
Sparse Core Ops, SparseCore 0:
  16.9 32.9 all-reduce.13
  53.4 32.2 all-reduce.15
  88.6 91.5 all-reduce.17
  182.5 64.9 all-reduce.19
